TPU v7x, 128 devices: a whole 4x4x4 slice. The times are simulated.
128 devices in a mesh: sess: 16 (over z, x), act: 8 (over y, core).
Axes of the slice: x: 4, y: 4, z: 4, core: 2. Of those that a mesh axis runs over, the one named last changes fastest.
Arguments:
- hist: bfloat16 [8192, 131072], P('sess', 'act'), may hold values from 0.049804688 to 5
- tile_mask: int32 [64, 1024], P('sess', 'act'), may hold values 0 or 1
- planes: bfloat16 [131072, 1024], P('act', 'sess'), may hold values from -0.015625 to 0.015625
- pairs: int32 [256, 2], P('sess'), may hold values from 0 to 63
Outputs:
- scores: float32 [256, 128, 128], P(('sess', 'act'))
All inputs are finite; a program needn't handle non-finite values. No bound on the sum of `tile_mask` on one device may be relied on, other than what follows from the above.
Results may differ from a plain program's by a relative error of at most 0.0003.
Values may be sent and summed in bfloat16 or wider, within the bound.
A program may use at most 192 MiB of HBM per device.

v0:
```python
import jax
import jax.numpy as jnp
from jax import lax
from jax.sharding import PartitionSpec as P

P_SIZE = 1024


def own_share(values, count):
    place = lax.axis_index("act")
    return lax.dynamic_slice_in_dim(values, place * count, count, 0)


def body(hist, tile_mask, planes, pairs):
    rows, acts = hist.shape
    row_blocks, act_blocks = tile_mask.shape
    blk = rows // row_blocks
    planes_all = P_SIZE
    masked = (
        hist.reshape(row_blocks, blk, act_blocks, blk)
        * tile_mask.astype(jnp.bfloat16)[:, None, :, None]
    ).reshape(rows, acts)
    partial_proj = jnp.dot(
        masked,
        lax.all_gather(planes, "sess", axis=1, tiled=True),
        preferred_element_type=jnp.float32,
    )
    proj = lax.psum_scatter(partial_proj, "act", scatter_dimension=1, tiled=True)
    share = proj.shape[1]
    pair_count = pairs.shape[0]
    own_count = pair_count // lax.axis_size("act")
    left_ids = pairs[:, 0]
    right_ids = pairs[:, 1]
    local_sq = lax.psum(jnp.sum(proj * proj, axis=1), "act")
    everyone, every_sq = (
        lax.all_gather(proj, "sess", axis=0, tiled=True),
        lax.all_gather(local_sq, "sess", axis=0, tiled=True),
    )
    blocks = everyone.reshape(-1, blk, share)
    norm_rows = every_sq.reshape(-1, blk)
    lefts = blocks[left_ids]
    rights = blocks[right_ids]
    dots = jnp.einsum("kuc,kvc->kuv", lefts, rights, precision=lax.Precision.HIGHEST)
    summed = lax.psum(dots, "act")
    dots_own = own_share(summed, own_count)
    left_sq = own_share(norm_rows[left_ids], own_count)
    right_sq = own_share(norm_rows[right_ids], own_count)
    left_scale = lax.rsqrt(left_sq / planes_all + 1e-06)
    right_scale = lax.rsqrt(right_sq / planes_all + 1e-06)
    return dots_own / planes_all * left_scale[:, :, None] * right_scale[:, None, :]


def solution(mesh):
    placed = (P("sess", "act"), P("sess", "act"), P("act", "sess"), P("sess", None))
    return jax.shard_map(
        body, mesh=mesh, in_specs=placed, out_specs=P(("sess", "act"), None, None), check_vma=False
    )
```

profile of v0, /device:TPU:1, one launch (start us, length us, event | category | flops | bytes accessed | tf_op | source)
XLA Modules:
  0.0 409.0 jit_solution(13980760528019967815)
XLA Ops:
  6.5 0.0 all-gather.4.cloned.1.call-start
  6.5 0.7 all-gather.4.cloned.1.call-update
  7.3 0.0 reduce-scatter.2.cloned.1.call-start
  7.3 0.7 convert_element_type.3
  8.0 201.7 %all-gather.4.cloned.1.call-done = bf16[16384,1024]{0,1:T(8,128)(2,1)} async-done(((bf16[16384,64]{0,1:T(8,128)(2,1)}), bf16[16384,1024]{0,1:T(8,128)(2,1)}) %all-gather.4.cloned.1.call-update) | async-done | bytes 33554448 | tf_op jit(solution)/shard_map/all_gather | solution.py:25
  209.7 6.6 %mul.37 = bf16[4,128,128,128]{3,2,1,0:T(8,128)(2,1)} broadcast(bf16[4,128]{1,0:T(4,128)(2,1)S(1)} %convert_element_type.3), dimensions={0,2} | broadcast | bytes 16778240 | tf_op jit(solution)/shard_map/mul | solution.py:20
  216.3 0.0 copy-start
  216.3 28.8 %fusion = f32[512,1024]{1,0:T(8,128)} fusion(bf16[16384,1024]{0,1:T(8,128)(2,1)} %all-gather.4.cloned.1.call-done, bf16[512,16384]{1,0:T(8,128)(2,1)} %param.4, bf16[64,8,128,128]{3,2,1,0:T(8,128)(2,1)} %bitcast.15), kind=kOutput, calls=%fused_computation.5 | convolution fusion | flops 17188257792 | bytes 69206016 | tf_op jit(solution)/shard_map/dot_general | solution.py:23
  245.1 0.0 reduce-scatter.2.cloned.1.call-update
  245.1 0.0 all-gather.6.cloned.1.call-start
  245.2 30.8 %reduce-scatter.2.cloned.1.call-done = f32[512,128]{1,0:T(8,128)} async-done(((f32[512,1024]{1,0:T(8,128)}), f32[512,128]{1,0:T(8,128)}) %reduce-scatter.2.cloned.1.call-update) | async-done | bytes 262160 | tf_op jit(solution)/shard_map/reduce_scatter | solution.py:28
  276.0 0.0 all-gather.6.cloned.1.call-update
  276.0 0.0 all-reduce.2.cloned.1.call-start
  276.1 0.0 copy-done
  276.1 55.0 %all-gather.6.cloned.1.call-done = f32[8192,128]{1,0:T(8,128)} async-done(((f32[512,128]{1,0:T(8,128)}), f32[8192,128]{1,0:T(8,128)}) %all-gather.6.cloned.1.call-update) | async-done | bytes 4194320 | tf_op jit(solution)/shard_map/all_gather | solution.py:36
  331.1 2.8 gather_fusion
  334.0 2.8 gather_fusion.1
  336.8 3.3 fusion.4
  340.1 0.0 all-reduce.2.cloned.1.call-update
  340.1 1.1 multiply_reduce_fusion
  341.2 12.6 %psum.15 = f32[512]{0:T(512)S(1)} all-reduce(f32[512]{0:T(512)S(1)} %multiply_reduce_fusion), channel_id=1, replica_groups=mesh['sess'=16,'act'=8] {'act'}, use_global_device_ids=true, to_apply=%region_3.0 | all-reduce | flops 512 | bytes 4096 | tf_op jit(solution)/shard_map/psum | solution.py:34
  353.8 18.4 %all-gather = f32[16,1,512]{2,1,0:T(1,128)S(1)} all-gather(f32[1,1,512]{2,1,0:T(1,128)S(1)} %bitcast.20), channel_id=1, replica_groups=mesh['sess'=16,'act'=8] {'sess'}, dimensions={0}, use_global_device_ids=true | all-gather | bytes 34816 | tf_op jit(solution)/shard_map/all_gather | solution.py:37
  372.2 0.6 gather_fusion.3
  372.8 0.6 gather_fusion.2
  373.4 27.4 %all-reduce.2.cloned.1.call-done = f32[16,128,128]{2,1,0:T(8,128)} async-done(((f32[16,128,128]{2,1,0:T(8,128)}), f32[16,128,128]{2,1,0:T(8,128)}) %all-reduce.2.cloned.1.call-update) | async-done | bytes 1048592 | tf_op jit(solution)/shard_map/psum | solution.py:44
  400.8 1.7 multiply_multiply_fusion
  (4 shorter events, 0.0 us)
Async XLA Ops:
  6.5 203.1 %all-gather.4.cloned.1.call-start = ((), (), s32[]{:S(2)}) async-start(), calls=%async_computation.1 | async-start | bytes 35651584 | tf_op jit(solution)/shard_map/all_gather | solution.py:25
  7.3 268.8 %reduce-scatter.2.cloned.1.call-start = ((), (), s32[]{:S(2)}) async-start(), calls=%async_computation.2 | async-start | bytes 2359296 | tf_op jit(solution)/shard_map/reduce_scatter | solution.py:28
  216.3 59.8 %copy-start = (s32[16,2]{0,1:T(2,128)S(1)}, s32[16,2]{0,1:T(2,128)}, u32[]{:S(2)}) copy-start(s32[16,2]{0,1:T(2,128)} %param.7) | copy-start | bytes 388
  245.1 86.0 %all-gather.6.cloned.1.call-start = ((), (), s32[]{:S(2)}) async-start(), calls=%async_computation.3 | async-start | bytes 4456448 | tf_op jit(solution)/shard_map/all_gather | solution.py:36
  276.0 124.8 %all-reduce.2.cloned.1.call-start = ((), (), s32[]{:S(2)}) async-start(), calls=%async_computation.4 | async-start | bytes 2097152 | tf_op jit(solution)/shard_map/psum | solution.py:44
Sparse Core Ops, SparseCore 0:
  9.5 200.1 all-gather.3
  245.2 30.7 reduce-scatter.1
  278.2 52.9 all-gather.5
  340.2 60.5 all-reduce.1
where the time goes:
time: 411 us; the launch traced here: 409 us
  waiting for transfers between devices  316 us (77%)
  matrix products  32.1 us (8%)
  blocking collectives  31 us (8%)
  local copies, waits for them, and re-layouts  13.4 us (3%)
  between operations  13.2 us (3%)
    all_gather x1, waiting for transfers between devices, body(): lax.all_gather(planes, 'sess', axis=1, tiled=True)  202 us
    all_gather x1, waiting for transfers between devices, body(): lax.all_gather(proj, 'sess', axis=0, tiled=True)  55 us
    reduce_scatter x1, waiting for transfers between devices, body(): lax.psum_scatter(partial_proj, 'act', scatter_dimension=1, tiled=True)  30.8 us
    dot_general x1, matrix products, body(): jnp.dot(masked, lax.all_gather(planes, 'sess', axis=1, tiled=True), prefe...  28.8 us
    psum x1, waiting for transfers between devices, body(): summed = lax.psum(dots, 'act')  27.4 us
    all_gather x1, blocking collectives, body(): lax.all_gather(local_sq, 'sess', axis=0, tiled=True)  18.4 us
    psum x1, blocking collectives, body(): local_sq = lax.psum(jnp.sum(proj * proj, axis=1), 'act')  12.6 us
  transfers between devices with their start and end apart: 4, of which 4 were waited for; matrix products, arithmetic and copies ran while one was open for 1% of the time, Pallas kernels for 0%

commit v1 on v0

v1 whole, which is shorter than its diff:
```python
import heapq

import jax
import jax.numpy as jnp
from jax import lax
from jax.experimental import pallas as pl
from jax.experimental.pallas import tpu as pltpu
from jax.sharding import PartitionSpec as P

MESH = pl.DeviceIdType.MESH
P_SIZE = 1024
RING = 4
UNITS = 4
BLK = 128
KC = 2048


def plan(units, depth, length, latency):
    todo = []
    for u in range(units):
        for s in (1, -1):
            for hop in (1, 2):
                todo.append((u, 0, 0, s, hop))
                todo += [(u, 1, dp, s, hop) for dp in (0, -1, 1, 2)]

    def needs(c):
        u, stage, dp, s, hop = c
        if hop == 2:
            return [(u, stage, dp, s, 1)]
        if stage == 0 or dp == 0:
            return []
        if dp == 2:
            return [(u, 0, 0, 1, 2), (u, 0, 0, -1, 2)]
        return [(u, 0, 0, -dp, 1)]

    def rank(c):
        u, stage, dp, s, hop = c
        far = {2: 2, -1: 1, 1: 1, 0: 0}[dp]
        return (u // 2, stage, hop if stage == 0 else 0, far, hop, u, s)

    todo.sort(key=rank)
    done, events, flying, free, count = set(), [], {}, {}, 0

    def start(now):
        nonlocal count
        out = []
        for c in todo:
            if not all(d in done for d in needs(c)):
                continue
            link = ((c[0] + c[1]) % 2, c[3])
            flying[link] = [f for f in flying.get(link, []) if f > now]
            if len(flying[link]) >= depth:
                continue
            end = max(now, free.get(link, 0.0)) + length / c[4]
            free[link] = end
            flying[link].append(end)
            heapq.heappush(events, (end + latency, count, c))
            count += 1
            out.append(c)
        for c in out:
            todo.remove(c)
        return out

    order = [(None, start(0.0))]
    while events:
        now, _, c = heapq.heappop(events)
        done.add(c)
        order.append((c, start(now)))
    assert not todo
    return order


GATHER = plan(UNITS, 3, 11.3, 2.0)
SPREAD = plan(2, 20, 1.4, 2.0)


def numbered(order):
    ids = {}
    for _, started in order:
        for c in started:
            ids[c] = len(ids)
    return ids


GATHER_IDS = numbered(GATHER)
SPREAD_IDS = numbered(SPREAD)


def arrivals(c):
    u, stage, dp, s, hop = c
    back = -s if hop == 1 else 2
    return (u, back, 0) if stage == 0 else (u, dp, back)


def kernel(
    planes, hist, mask, pairs, out,
    g_ref, h_ref, acc, r1, r2, pb, d_ref, e1, e2,
    own_sem, hist_sem, send, recv, s1, v1, s2, v2, s3, v3, ts, tv, us, uv,
):
    depth = planes.shape[1]
    half = depth // 2
    cols = planes.shape[0] // UNITS
    me = lax.axis_index("sess")
    z, x = me // RING, me % RING
    act = lax.axis_index("act")
    y, core = act // 2, act % 2
    place = (z, x)

    def wrap(v, d):
        return lax.rem(v + d + RING, RING)

    def near(axis, d):
        return {"sess": wrap(z, d) * RING + x if axis == 0 else z * RING + wrap(x, d)}

    def along_y(d):
        return {"act": wrap(y, d) * 2 + core}

    twin = {"act": y * 2 + 1 - core}

    def remote(src, dst, send_sem, recv_sem, device):
        return pltpu.make_async_remote_copy(
            src_ref=src, dst_ref=dst, send_sem=send_sem, recv_sem=recv_sem,
            device_id=device, device_id_type=MESH,
        )

    peers = [near(a, d) for a in (0, 1) for d in (1, -1)]
    peers += [along_y(d) for d in (1, -1, 2)] + [twin]
    barrier = pltpu.get_barrier_semaphore()
    for peer in peers:
        pl.semaphore_signal(barrier, inc=1, device_id=peer, device_id_type=MESH)

    owns = []
    for u in range(UNITS):
        pc, qc = place[u % 2], place[1 - u % 2]
        own = pltpu.make_async_copy(
            planes.at[pl.ds(u * cols, cols)], g_ref.at[u, qc * RING + pc], own_sem.at[u]
        )
        own.start()
        owns.append(own)
    load = pltpu.make_async_copy(hist, h_ref, hist_sem)
    load.start()
    pl.semaphore_wait(barrier, len(peers))
    for own in owns:
        own.wait()

    def ends(c):
        u, stage, dp, s, hop = c
        pc, qc = place[u % 2], place[1 - u % 2]
        axis = (u + stage) % 2
        if stage == 0:
            return pc if hop == 1 else wrap(pc, -s), qc, near(axis, s)
        return wrap(pc, dp), qc if hop == 1 else wrap(qc, -s), near(axis, s)

    def gather_copy(c):
        p, q, device = ends(c)
        ref = g_ref.at[c[0], q * RING + p]
        if c[4] == 2:
            ref = ref.at[:, pl.ds(0 if c[3] == 1 else half, half)]
        i = GATHER_IDS[c]
        return remote(ref, ref, send.at[i], recv.at[i], device)

    def spread_copy(h, c):
        p, q, device = ends(c)
        at = (p * RING + q if c[0] == 0 else q * RING + p) * RING
        if c[4] == 2:
            rows = pl.ds(at if c[3] == 1 else at + 2, 2)
        else:
            rows = pl.ds(at, 4)
        ref = pb.at[rows, pl.ds((2 * h + c[0]) * 32, 32)]
        i = SPREAD_IDS[c]
        return remote(ref, ref, ts.at[h, i], tv.at[h, i], device)

    def batch(u, dq):
        q = wrap(place[1 - u % 2], dq)

        def step(i, total):
            at = pl.ds(pl.multiple_of(i * KC, KC), KC)
            some = g_ref[u, pl.ds(q * RING, RING), :, at].reshape(RING * cols, KC)
            return total + lax.dot_general(
                some, h_ref[:, at], (((1,), (1,)), ((), ())),
                preferred_element_type=jnp.float32,
            )

        rows = h_ref.shape[0]
        total = lax.fori_loop(0, depth // KC, step, jnp.zeros((RING * cols, rows), jnp.float32))
        acc[u, q // 2, pl.ds((q % 2) * 2, 2)] = total.reshape(2, 2 * cols, rows)

    def pair_copy(u):
        return remote(acc.at[u, 1 - core], r1.at[u], s1.at[u], v1.at[u], twin)

    def ring_copy(u, d):
        i = {1: 0, -1: 1, 2: 2}[d]
        return remote(acc.at[u, core, wrap(y, d)], r2.at[u, i], s2.at[u, i], v2.at[u, i], along_y(d))

    def reduce_second(u):
        pair_copy(u).wait_recv()
        acc[u, core] = acc[u, core] + r1[u]
        for d in (2, 1, -1):
            ring_copy(u, d).start()

    def reduce_third(u):
        for d in (1, -1, 2):
            ring_copy(u, d).wait_recv()
        total = acc[u, core, y] + r2[u, 0] + r2[u, 1] + r2[u, 2]
        for b in range(4):
            pb[me * RING + b, pl.ds(u * 32, 32)] = total[:, b * BLK : (b + 1) * BLK]

    masked = False
    arrived = {(u, dp, dq): 0.0 for u in range(UNITS) for dp in (0, 1, -1, 2) for dq in (0, 1, -1, 2)}
    for u in range(UNITS):
        arrived[u, 0, 0] = 1.0
    ready = []
    left = {u: 4 for u in range(UNITS)}
    later = []
    for n, (c, started) in enumerate(GATHER):
        if c is not None:
            gather_copy(c).wait_recv()
            u, dp, dq = arrivals(c)
            arrived[u, dp, dq] += 1.0 if c[4] == 1 else 0.5
            if all(arrived[u, d, dq] == 1.0 for d in (0, 1, -1, 2)):
                ready.append((u, dq))
        for c in started:
            gather_copy(c).start()
        if not masked:
            load.wait()
            masked = True

            def tile(i, _):
                at = pl.ds(pl.multiple_of(i * BLK, BLK), BLK)
                for r in range(mask.shape[0]):
                    keep = mask[r, i].astype(jnp.float32).astype(jnp.bfloat16)
                    rows = pl.ds(r * BLK, BLK)
                    h_ref[rows, at] = h_ref[rows, at] * keep
                return 0

            lax.fori_loop(0, mask.shape[1], tile, 0)
        for due, do in [e for e in later if e[0] <= n]:
            do()
        later = [e for e in later if e[0] > n]
        for u, dq in ready:
            batch(u, dq)
            left[u] -= 1
            if left[u] == 0:
                pair_copy(u).start()
                later.append((n + 3, lambda u=u: reduce_second(u)))
                later.append((n + 7, lambda u=u: reduce_third(u)))
        ready = []

    def spread_step(h, n):
        c, started = SPREAD[n]
        if c is not None:
            spread_copy(h, c).wait_recv()
        for c in started:
            spread_copy(h, c).start()

    spread_step(0, 0)
    for n in range(1, 9):
        spread_step(0, n)
    later.sort(key=lambda e: e[0])
    for _, do in later[:2]:
        do()
    for n in range(9, 25):
        spread_step(0, n)
    for _, do in later[2:]:
        do()
    spread_step(1, 0)
    for n in range(25, len(SPREAD)):
        spread_step(0, n)
    for n in range(1, len(SPREAD)):
        spread_step(1, n)

    def one_pair(k, _):
        lt = pb[pairs[k, 0]]
        rt = pb[pairs[k, 1]]
        dots = lax.dot_general(
            lt, rt, (((0,), (0,)), ((), ())),
            precision=lax.Precision.HIGHEST, preferred_element_type=jnp.float32,
        )
        at = d_ref.at[(k // 2) % 2, k // 4, k % 2]
        at[0:BLK] = dots
        at[BLK : BLK + 8] = jnp.broadcast_to(jnp.sum(lt * lt, axis=0, keepdims=True), (8, BLK))
        at[BLK + 8 : BLK + 16] = jnp.broadcast_to(jnp.sum(rt * rt, axis=0, keepdims=True), (8, BLK))
        return 0

    lax.fori_loop(0, pairs.shape[0], one_pair, 0)
    swap = remote(d_ref.at[1 - core], e1, s3, v3, twin)
    swap.start()
    swap.wait_recv()

    def add(i, _):
        d_ref[core, i] = d_ref[core, i] + e1[i]
        return 0

    lax.fori_loop(0, RING, add, 0)

    def share_copy(d):
        i = {1: 0, -1: 1, 2: 2}[d]
        return remote(d_ref.at[core, wrap(y, d)], e2.at[i], us.at[i], uv.at[i], along_y(d))

    for d in (2, 1, -1):
        share_copy(d).start()
    for d in (1, -1, 2):
        share_copy(d).wait_recv()
    for j in range(2):
        total = d_ref[core, y, j] + e2[0, j] + e2[1, j] + e2[2, j]
        lscale = lax.rsqrt(total[BLK : BLK + 1] / P_SIZE + 1e-06)
        rscale = lax.rsqrt(total[BLK + 8 : BLK + 9] / P_SIZE + 1e-06)
        lfull = jnp.broadcast_to(lscale, (BLK, BLK)).T
        out[j] = total[0:BLK] / P_SIZE * lfull * rscale

    for c in GATHER_IDS:
        gather_copy(c).wait_send()
    for h in range(2):
        for c in SPREAD_IDS:
            spread_copy(h, c).wait_send()
    for u in range(UNITS):
        pair_copy(u).wait_send()
        for d in (1, -1, 2):
            ring_copy(u, d).wait_send()
    swap.wait_send()
    for d in (1, -1, 2):
        share_copy(d).wait_send()


def body(hist, tile_mask, planes, pairs):
    rows, depth = hist.shape
    cols = planes.shape[1] // UNITS
    f32 = jnp.float32
    dma = pltpu.SemaphoreType.DMA
    return pl.pallas_call(
        kernel,
        out_shape=jax.ShapeDtypeStruct((2, BLK, BLK), f32),
        in_specs=[
            pl.BlockSpec(memory_space=pl.ANY),
            pl.BlockSpec(memory_space=pl.ANY),
            pl.BlockSpec(memory_space=pltpu.SMEM),
            pl.BlockSpec(memory_space=pltpu.SMEM),
        ],
        out_specs=pl.BlockSpec(memory_space=pltpu.VMEM),
        scratch_shapes=[
            pltpu.VMEM((UNITS, RING * RING, cols, depth), jnp.bfloat16),
            pltpu.VMEM((rows, depth), jnp.bfloat16),
            pltpu.VMEM((UNITS, 2, RING, 2 * cols, rows), f32),
            pltpu.VMEM((UNITS, RING, 2 * cols, rows), f32),
            pltpu.VMEM((UNITS, 3, 2 * cols, rows), f32),
            pltpu.VMEM((RING * RING * RING, BLK, BLK), f32),
            pltpu.VMEM((2, RING, 2, BLK + 16, BLK), f32),
            pltpu.VMEM((RING, 2, BLK + 16, BLK), f32),
            pltpu.VMEM((3, 2, BLK + 16, BLK), f32),
            dma((UNITS,)),
            dma,
            dma((len(GATHER_IDS),)),
            dma((len(GATHER_IDS),)),
            dma((UNITS,)),
            dma((UNITS,)),
            dma((UNITS, 3)),
            dma((UNITS, 3)),
            dma,
            dma,
            dma((2, len(SPREAD_IDS))),
            dma((2, len(SPREAD_IDS))),
            dma((3,)),
            dma((3,)),
        ],
        compiler_params=pltpu.CompilerParams(
            collective_id=0, has_side_effects=True, vmem_limit_bytes=63 * 2**20
        ),
    )(planes.T, hist, tile_mask, pairs)


def solution(mesh):
    placed = (P("sess", "act"), P("sess", "act"), P("act", "sess"), P("sess", None))
    return jax.shard_map(
        body, mesh=mesh, in_specs=placed, out_specs=P(("sess", "act"), None, None), check_vma=False
    )
```

time: 411 us -> 257 us (0.63)
  waiting for transfers between devices: 316 us -> 0 us
  Pallas kernels: 0 us -> 253 us
  matrix products: 32.1 us -> 0 us
  blocking collectives: 31 us -> 0 us
  between operations: 13.2 us -> 0.01 us
  local copies, waits for them, and re-layouts: 13.4 us -> 2.92 us
    all_gather x2 -> x0, waiting for transfers between devices: 257 us -> none  [the longest x1 202 us: body(): lax.all_gather(planes, 'sess', axis=1, tiled=True)]
    pallas_call x0 -> x1, Pallas kernels: none -> 253 us  [body(): pl.pallas_call(kernel, out_shape=jax.ShapeDtypeStruct((2, BLK, BLK), f32)...]
    dot_general x2 -> x0, matrix products: 32.1 us -> none  [the longest x1 28.8 us: body(): jnp.dot(masked, lax.all_gather(planes, 'sess', axis=1, tiled=True), prefe...]
    reduce_scatter x1 -> x0, waiting for transfers between devices: 30.8 us -> none  [body(): lax.psum_scatter(partial_proj, 'act', scatter_dimension=1, tiled=True)]
    psum x1 -> x0, waiting for transfers between devices: 27.4 us -> none  [body(): summed = lax.psum(dots, 'act')]
    all_gather x1 -> x0, blocking collectives: 18.4 us -> none  [body(): lax.all_gather(local_sq, 'sess', axis=0, tiled=True)]
    psum x1 -> x0, blocking collectives: 12.6 us -> none  [body(): local_sq = lax.psum(jnp.sum(proj * proj, axis=1), 'act')]
    gather x4 -> x0, local copies, waits for them, and re-layouts: 6.73 us -> none  [the longest x1 2.8 us: body(): rights = blocks[right_ids]]
  transfers between devices with their start and end apart: 4 -> 0, of which waited for: 4 -> 0; matrix products, arithmetic and copies ran while one was open for 1% -> 0% of each run, Pallas kernels for 0% -> 0%
where the time goes in v1:
time: 257 us; the launch traced here: 256 us
  Pallas kernels  253 us (98%)
  local copies, waits for them, and re-layouts  2.92 us (1%)
    pallas_call x1, Pallas kernels, body(): pl.pallas_call(kernel, out_shape=jax.ShapeDtypeStruct((2, BLK, BLK), f32)...  253 us

profile of v1, /device:TPU:1, one launch (start us, length us, event | category | flops | bytes accessed | tf_op | source)
XLA Modules:
  0.0 256.4 jit_solution(401419311796127131)
XLA Ops:
  0.0 1.4 copy.5.pairs
  1.4 253.5 %shard_map.46 = f32[2,128,128]{2,1,0:T(8,128)} custom-call(bf16[64,16384]{1,0:T(8,128)(2,1)} %bitcast.1, bf16[512,16384]{1,0:T(8,128)(2,1)} %hist.1, s32[4,128]{1,0:T(4,128)} %mask.1, s32[16,2]{1,0:T(8,128)} %copy.5.pairs), custom_call_target="tpu_custom_call" | custom-call | tf_op jit(solution)/shard_map/pallas_call | solution.py:330
  254.9 1.6 copy.7

commit v2 on v1

v2 whole, which is shorter than its diff:
```python
import heapq

import jax
import jax.numpy as jnp
from jax import lax
from jax.experimental import pallas as pl
from jax.experimental.pallas import tpu as pltpu
from jax.sharding import PartitionSpec as P

MESH = pl.DeviceIdType.MESH
P_SIZE = 1024
RING = 4
UNITS = 4
BLK = 128
WAIT_PARTNER = 8
WAIT_HOME = 12


def simulate(todo, needs, rank, link, length, depth, latency=2.0, ready=()):
    todo = sorted(todo, key=rank)
    done, flying, free, count = set(), {}, {}, len(ready)
    events = [(at, i, mark) for i, (at, mark) in enumerate(ready)]
    heapq.heapify(events)

    def start(now):
        nonlocal count
        out = []
        for c in todo:
            if not all(d in done for d in needs(c)):
                continue
            way = link(c)
            flying[way] = [f for f in flying.get(way, []) if f > now]
            if len(flying[way]) >= depth:
                continue
            end = max(now, free.get(way, 0.0)) + length(c)
            free[way] = end
            flying[way].append(end)
            heapq.heappush(events, (end + latency, count, c))
            count += 1
            out.append(c)
        for c in out:
            todo.remove(c)
        return out

    order = [(None, start(0.0))]
    while events:
        now, _, c = heapq.heappop(events)
        done.add(c)
        order.append((c, start(now)))
    assert not todo
    simulate.end = now
    return order


MATE, PARTNER = 0, 1
MASKED = (-1, 0, 0, 0, 0)


def plan_gather():
    todo = [(k, 2, r, PARTNER, 1) for k in (0, 1) for r in range(4)]
    for u in range(2 * UNITS):
        todo += [(u, 0, 1, PARTNER, 1), (u, 0, 2, MATE, 1), (u, 0, 3, MATE, 1)]
        todo += [(u, 1, a, w, hop) for a in range(4) for w in (0, 1) for hop in (1, 2)]

    def needs(c):
        u, stage, a, w, hop = c
        if stage == 2:
            return [MASKED]
        if stage == 0:
            return [(u, 0, 1, PARTNER, 1)] if a == 3 else []
        if hop == 2:
            return [(u, 1, a, 1 - w, 1)]
        return [(u, 0, a, PARTNER if a == 1 else MATE, 1)] if a else []

    def rank(c):
        u, stage, a, w, hop = c
        if stage == 2:
            return (HIST_RANK[a], -1, a, 0, 0, u)
        return (u // 2, stage, a if stage == 0 else 0, 0 if stage == 0 else -a, hop, w, u)

    def link(c):
        u, stage, a, w, hop = c
        return (u + (stage == 1)) % 2

    def length(c):
        return 11.4 * (1.0 if c[1] == 2 else 0.125 / c[4])

    return simulate(todo, needs, rank, link, length, DEPTH, ready=[(9.0, MASKED)])


def plan_spread():
    todo = []
    for u in (0, 1):
        for s in (1, -1):
            for hop in (1, 2):
                todo.append((u, 0, 0, s, hop))
                todo += [(u, 1, dp, s, hop) for dp in (0, -1, 1, 2)]

    def needs(c):
        u, stage, dp, s, hop = c
        if hop == 2:
            return [(u, stage, dp, s, 1)]
        if stage == 0 or dp == 0:
            return []
        if dp == 2:
            return [(u, 0, 0, 1, 2), (u, 0, 0, -1, 2)]
        return [(u, 0, 0, -dp, 1)]

    def rank(c):
        u, stage, dp, s, hop = c
        far = {2: 2, -1: 1, 1: 1, 0: 0}[dp]
        return (stage, hop if stage == 0 else 0, far, hop, u, s)

    def link(c):
        return ((c[0] + c[1]) % 2, c[3])

    return simulate(todo, needs, rank, link, lambda c: 1.4 / c[4], 20)


HIST_RANK = (0, 0, 0, 0)
DEPTH = 10
GATHER = plan_gather()
SPREAD = plan_spread()
DIRECT = (UNITS - 1,)
PARTS = ((0, 96), (96, 32))


def numbered(order):
    ids = {}
    for _, started in order:
        for c in started:
            ids[c] = len(ids)
    return ids


GATHER_IDS = numbered(GATHER)
SPREAD_IDS = numbered(SPREAD)


def kernel(
    planes, hist, mask, pairs, out,
    g_ref, h_ref, hp, acc, accp, r1, r2, r3, r4, r5, pb, d_ref, e1, e2,
    own_sem, hist_sem, send, recv, s1, v1, s2, v2, s3, v3, s4, v4, s5, v5, s6, v6,
    ts, tv, us, uv,
):
    cols, depth = planes.shape[1:]
    half, quarter = depth // 2, depth // 4
    rows = h_ref.shape[0]
    me = lax.axis_index("sess")
    z, x = me // RING, me % RING
    act = lax.axis_index("act")
    y, core = act // 2, act % 2
    place = (z, x)

    def wrap(v, d):
        return lax.rem(v + d + RING, RING)

    def near(axis, d):
        return {"sess": wrap(z, d) * RING + x if axis == 0 else z * RING + wrap(x, d)}

    def along_y(d):
        return {"act": wrap(y, d) * 2 + core}

    twin = {"act": y * 2 + 1 - core}

    def remote(src, dst, send_sem, recv_sem, device):
        return pltpu.make_async_remote_copy(
            src_ref=src, dst_ref=dst, send_sem=send_sem, recv_sem=recv_sem,
            device_id=device, device_id_type=MESH,
        )

    def toward(axis, way):
        even = 1 - 2 * lax.rem(place[axis] + core, 2)
        return even if way == MATE else -even

    def beside(axis, way):
        return near(axis, toward(axis, way))

    group = [lax.rem(place[k] - core + RING, RING) // 2 for k in (0, 1)]
    keep_at = [pl.multiple_of(k * half + group[k] * quarter, quarter) for k in (0, 1)]
    give_at = [pl.multiple_of(k * half + (1 - group[k]) * quarter, quarter) for k in (0, 1)]

    around = [(a, d) for a in (0, 1) for d in (1, -1)]
    peers = [near(a, d) | {"act": y * 2 + c} for a, d in around for c in (0, 1)]
    peers += [along_y(d) for d in (1, -1, 2)] + [twin]
    barrier = pltpu.get_barrier_semaphore()
    for peer in peers:
        pl.semaphore_signal(barrier, inc=1, device_id=peer, device_id_type=MESH)

    pieces = give_at + keep_at
    loads = []
    for i, at in enumerate(pieces):
        at = pl.ds(at, quarter)
        loads.append(pltpu.make_async_copy(hist.at[:, at], h_ref.at[:, at], hist_sem.at[i]))
        loads[i].start()
    owns = []
    for k in (0, 1):
        src = planes.at[:, :, pl.ds(keep_at[k], quarter)]
        owns.append(pltpu.make_async_copy(src, g_ref.at[:, k, me], own_sem.at[k]))
        owns[k].start()
    pl.semaphore_wait(barrier, len(peers))

    def mask_piece(i):
        loads[i].wait()
        first = pieces[i] // BLK

        def tile(j, _):
            at = pl.ds(pl.multiple_of(pieces[i] + j * BLK, BLK), BLK)
            for r in range(mask.shape[0]):
                keep = mask[r, first + j].astype(jnp.float32).astype(jnp.bfloat16)
                some = pl.ds(r * BLK, BLK)
                h_ref[some, at] = h_ref[some, at] * keep
            return 0

        lax.fori_loop(0, quarter // BLK, tile, 0)

    def ends(c):
        u, stage, dp, s, hop = c
        pc, qc = place[u % 2], place[1 - u % 2]
        axis = (u + stage) % 2
        if stage == 0:
            return pc if hop == 1 else wrap(pc, -s), qc, near(axis, s)
        return wrap(pc, dp), qc if hop == 1 else wrap(qc, -s), near(axis, s)

    def slot(c, p, q):
        return p * RING + q if c[0] % 2 == 0 else q * RING + p

    def gather_copy(c):
        u, stage, a, w, hop = c
        i = GATHER_IDS[c]
        g, k = u // 2, u % 2
        if stage == 2:
            some = pl.ds(a * BLK, BLK)
            src = h_ref.at[some, pl.ds(give_at[k], quarter)]
            return remote(src, hp.at[k, some], send.at[i], recv.at[i], beside(k, w))
        pc, qc = place[k], place[1 - k]
        axis = k if stage == 0 else 1 - k
        if stage == 0:
            p, q = wrap(pc, toward(k, PARTNER)) if a == 3 else pc, qc
        else:
            steps = (0, toward(k, PARTNER), toward(k, MATE), 2)
            p, q = wrap(pc, steps[a]), qc
            if hop == 2:
                q = wrap(qc, toward(1 - k, 1 - w))
        ref = g_ref.at[g, k, slot(c, p, q)]
        src = ref
        if hop == 2:
            ref = src = ref.at[:, pl.ds(w * quarter // 2, quarter // 2)]
        elif stage == 0 and a == 1:
            src = planes.at[g, :, pl.ds(give_at[k], quarter)]
        elif a == 0 or (stage == 0 and a == 2):
            src = planes.at[g, :, pl.ds(keep_at[k], quarter)]
        return remote(src, ref, send.at[i], recv.at[i], beside(axis, w))

    def spread_copy(h, c):
        p, q, device = ends(c)
        at = slot(c, p, q) * RING + 2 * c[0]
        if c[4] == 2:
            rows = pl.ds(at if c[3] == 1 else at + 1, 1)
        else:
            rows = pl.ds(at, 2)
        ref = pb.at[rows, pl.ds(*PARTS[h])]
        i = SPREAD_IDS[c]
        return remote(ref, ref, ts.at[h, i], tv.at[h, i], device)

    shape = (RING, 2, 2 * cols, rows)

    def multiply(g, k, first):
        some = g_ref[g, k].reshape(RING * RING * cols, quarter)
        dims = (((1,), (1,)), ((), ()))
        mine = h_ref[:, pl.ds(keep_at[k], quarter)]
        total = lax.dot_general(some, mine, dims, preferred_element_type=jnp.float32)
        total = total.reshape(shape)
        acc[g] = total if first else acc[g] + total

    def multiply_partner(g, k):
        some = g_ref[g, k].reshape(RING * RING * cols, quarter)
        dims = (((1,), (1,)), ((), ()))
        total = lax.dot_general(some, hp[k], dims, preferred_element_type=jnp.float32)
        accp[g, k] = total.reshape(shape)

    turn = {1: 0, -1: 1, 2: 2}

    def pair_copy(g):
        return remote(acc.at[g, :, 1 - core], r1.at[g], s1.at[g], v1.at[g], twin)

    def ring_copy(g, d):
        i = turn[d]
        src = acc.at[g, wrap(y, d), core]
        return remote(src, r2.at[g, i], s2.at[g, i], v2.at[g, i], along_y(d))

    def partner_ring(g, k, d):
        i = turn[d]
        src = accp.at[g, k, wrap(y, d)]
        return remote(src, r3.at[g, k, i], s4.at[g, k, i], v4.at[g, k, i], along_y(d))

    def home_copy(g, k, c):
        target = beside(k, PARTNER) | {"act": y * 2 + c}
        return remote(
            accp.at[g, k, y, c], r4.at[g, core, k], s5.at[g, k, c], v5.at[g, core, k], target
        )

    def home_wait(g, k, c):
        sem = v5.at[g, c, k]
        remote(r4.at[g, c, k], r4.at[g, c, k], s5.at[g, k, c], sem, twin).wait_recv()

    def direct_copy(k):
        return remote(accp.at[UNITS - 1, k], r5.at[k], s6.at[k], v6.at[k], beside(k, PARTNER))

    def reduce_first(g):
        if g in DIRECT:
            for k in (0, 1):
                direct_copy(k).wait_recv()
            acc[g] = acc[g] + r5[0] + r5[1]
        pair_copy(g).start()

    def reduce_second(g):
        pair_copy(g).wait_recv()
        acc[g, :, core] = acc[g, :, core] + r1[g]
        for d in (2, 1, -1):
            ring_copy(g, d).start()

    def reduce_partner(g):
        if g in DIRECT:
            return
        for k in (0, 1):
            for d in (1, -1, 2):
                partner_ring(g, k, d).wait_recv()
            accp[g, k, y] = accp[g, k, y] + r3[g, k, 0] + r3[g, k, 1] + r3[g, k, 2]
            for c in (0, 1):
                home_copy(g, k, c).start()

    def reduce_third(g):
        for d in (1, -1, 2):
            ring_copy(g, d).wait_recv()
        total = acc[g, y, core] + r2[g, 0] + r2[g, 1] + r2[g, 2]
        if g not in DIRECT:
            for k in (0, 1):
                for c in (0, 1):
                    home_wait(g, k, c)
                    total = total + r4[g, c, k]
        for b in range(4):
            pb[me * RING + b, pl.ds(g * 32, 32)] = total[:, b * BLK : (b + 1) * BLK]

    def spread_steps(h, begin, end):
        for c, started in SPREAD[begin:end]:
            if c is not None:
                spread_copy(h, c).wait_recv()
            for c2 in started:
                spread_copy(h, c2).start()

    got = {u: 1.0 for u in range(2 * UNITS)}
    tiles = {0: 0, 1: 0}
    waiting, seen, later = [], set(), []
    steps = len(SPREAD)
    last = max(n for n, (_, started) in enumerate(GATHER) if started)
    for n, (c, started) in enumerate(GATHER):
        if c == MASKED:
            mask_piece(0)
            mask_piece(1)
        elif c is not None:
            gather_copy(c).wait_recv()
            if c[1] == 2:
                tiles[c[0]] += 1
            else:
                got[c[0]] += 1.0 / c[4]
                if got[c[0]] == 16.0:
                    waiting.append(c[0])
        for c2 in started:
            gather_copy(c2).start()
        if c == MASKED:
            mask_piece(2)
            mask_piece(3)
            owns[0].wait()
            owns[1].wait()
        for due, do in [e for e in later if e[0] <= n]:
            do()
        later = [e for e in later if e[0] > n]
        if n == last:
            assert not later, later
            spread_steps(0, 0, 1)
        for u in [u for u in waiting if tiles[u % 2] == 4]:
            waiting.remove(u)
            g, k = u // 2, u % 2
            multiply_partner(g, k)
            if g in DIRECT:
                direct_copy(k).start()
            else:
                for d in (2, 1, -1):
                    partner_ring(g, k, d).start()
            multiply(g, k, g not in seen)
            if g in seen:
                if g in DIRECT:
                    assert n >= len(GATHER) - 4
                    later.append((n, lambda g=g: reduce_first(g)))
                else:
                    reduce_first(g)
                later.append((n + 4, lambda g=g: reduce_second(g)))
                later.append((n + WAIT_PARTNER, lambda g=g: reduce_partner(g)))
                later.append((n + WAIT_HOME, lambda g=g: reduce_third(g)))
            seen.add(g)

    later.sort(key=lambda e: e[0])
    assert not waiting and len(later) == 4
    later.pop(0)[1]()
    spread_steps(0, 1, 9)
    later[0][1]()
    spread_steps(0, 9, 25)
    later[2][1]()
    spread_steps(1, 0, 1)
    spread_steps(0, 25, steps)
    spread_steps(1, 1, steps)

    def one_pair(k, _):
        lt = pb[pairs[k, 0]]
        rt = pb[pairs[k, 1]]
        dots = lax.dot_general(
            lt, rt, (((0,), (0,)), ((), ())),
            precision=lax.Precision.HIGHEST, preferred_element_type=jnp.float32,
        )
        at = d_ref.at[(k // 2) % 2, k // 4, k % 2]
        at[0:BLK] = dots
        at[BLK : BLK + 8] = jnp.broadcast_to(jnp.sum(lt * lt, axis=0, keepdims=True), (8, BLK))
        at[BLK + 8 : BLK + 16] = jnp.broadcast_to(jnp.sum(rt * rt, axis=0, keepdims=True), (8, BLK))
        return 0

    lax.fori_loop(0, pairs.shape[0], one_pair, 0, unroll=4)
    swap = remote(d_ref.at[1 - core], e1, s3, v3, twin)
    swap.start()
    swap.wait_recv()

    def add(i, _):
        d_ref[core, i] = d_ref[core, i] + e1[i]
        return 0

    lax.fori_loop(0, RING, add, 0)

    def share_copy(d):
        i = {1: 0, -1: 1, 2: 2}[d]
        return remote(d_ref.at[core, wrap(y, d)], e2.at[i], us.at[i], uv.at[i], along_y(d))

    for d in (2, 1, -1):
        share_copy(d).start()
    for d in (1, -1, 2):
        share_copy(d).wait_recv()
    for j in range(2):
        total = d_ref[core, y, j] + e2[0, j] + e2[1, j] + e2[2, j]
        lscale = lax.rsqrt(total[BLK : BLK + 1] / P_SIZE + 1e-06)
        rscale = lax.rsqrt(total[BLK + 8 : BLK + 9] / P_SIZE + 1e-06)
        lfull = jnp.broadcast_to(lscale, (BLK, BLK)).T
        out[j] = total[0:BLK] / P_SIZE * lfull * rscale

    for c in GATHER_IDS:
        gather_copy(c).wait_send()
    for h in range(2):
        for c in SPREAD_IDS:
            spread_copy(h, c).wait_send()
    for g in range(UNITS):
        pair_copy(g).wait_send()
        for d in (1, -1, 2):
            ring_copy(g, d).wait_send()
        for k in (0, 1):
            if g in DIRECT:
                direct_copy(k).wait_send()
                continue
            for d in (1, -1, 2):
                partner_ring(g, k, d).wait_send()
            for c in (0, 1):
                home_copy(g, k, c).wait_send()
    swap.wait_send()
    for d in (1, -1, 2):
        share_copy(d).wait_send()


def body(hist, tile_mask, planes, pairs):
    rows, depth = hist.shape
    cols = planes.shape[1] // UNITS
    f32 = jnp.float32
    dma = pltpu.SemaphoreType.DMA
    return pl.pallas_call(
        kernel,
        out_shape=jax.ShapeDtypeStruct((2, BLK, BLK), f32),
        in_specs=[
            pl.BlockSpec(memory_space=pl.ANY),
            pl.BlockSpec(memory_space=pl.ANY),
            pl.BlockSpec(memory_space=pltpu.SMEM),
            pl.BlockSpec(memory_space=pltpu.SMEM),
        ],
        out_specs=pl.BlockSpec(memory_space=pltpu.VMEM),
        scratch_shapes=[
            pltpu.VMEM((UNITS, 2, RING * RING, cols, depth // 4), jnp.bfloat16),
            pltpu.VMEM((rows, depth), jnp.bfloat16),
            pltpu.VMEM((2, rows, depth // 4), jnp.bfloat16),
            pltpu.VMEM((UNITS, RING, 2, 2 * cols, rows), f32),
            pltpu.VMEM((UNITS, 2, RING, 2, 2 * cols, rows), f32),
            pltpu.VMEM((UNITS, RING, 2 * cols, rows), f32),
            pltpu.VMEM((UNITS, 3, 2 * cols, rows), f32),
            pltpu.VMEM((UNITS - 1, 2, 3, 2, 2 * cols, rows), f32),
            pltpu.VMEM((UNITS - 1, 2, 2, 2 * cols, rows), f32),
            pltpu.VMEM((2, RING, 2, 2 * cols, rows), f32),
            pltpu.VMEM((RING * RING * RING, BLK, BLK), f32),
            pltpu.VMEM((2, RING, 2, BLK + 16, BLK), f32),
            pltpu.VMEM((RING, 2, BLK + 16, BLK), f32),
            pltpu.VMEM((3, 2, BLK + 16, BLK), f32),
            dma((2,)),
            dma((4,)),
            dma((len(GATHER_IDS),)),
            dma((len(GATHER_IDS),)),
            dma((UNITS,)),
            dma((UNITS,)),
            dma((UNITS, 3)),
            dma((UNITS, 3)),
            dma,
            dma,
            dma((UNITS - 1, 2, 3)),
            dma((UNITS - 1, 2, 3)),
            dma((UNITS - 1, 2, 2)),
            dma((UNITS - 1, 2, 2)),
            dma((2,)),
            dma((2,)),
            dma((2, len(SPREAD_IDS))),
            dma((2, len(SPREAD_IDS))),
            dma((3,)),
            dma((3,)),
        ],
        compiler_params=pltpu.CompilerParams(
            collective_id=0, has_side_effects=True, vmem_limit_bytes=63 * 2**20
        ),
    )(planes.T.reshape(UNITS, cols, depth), hist, tile_mask, pairs)


def solution(mesh):
    placed = (P("sess", "act"), P("sess", "act"), P("act", "sess"), P("sess", None))
    return jax.shard_map(
        body, mesh=mesh, in_specs=placed, out_specs=P(("sess", "act"), None, None), check_vma=False
    )
```

time: 257 us -> 219 us (0.85)
  Pallas kernels: 253 us -> 216 us
    pallas_call x1, Pallas kernels: 253 us -> 216 us  [body(): pl.pallas_call(kernel, out_shape=jax.ShapeDtypeStruct((2, BLK, BLK), f32)...]
where the time goes in v2:
time: 219 us
  Pallas kernels  216 us (99%)
  local copies, waits for them, and re-layouts  2.92 us (1%)
    pallas_call x1, Pallas kernels, body(): pl.pallas_call(kernel, out_shape=jax.ShapeDtypeStruct((2, BLK, BLK), f32)...  216 us

profile of v2, /device:TPU:1, one launch (start us, length us, event | category | flops | bytes accessed | tf_op | source)
XLA Modules:
  0.0 218.8 jit_solution(15473935055665899969)
XLA Ops:
  0.0 1.4 copy.5.pairs
  1.4 215.9 %shard_map.46 = f32[2,128,128]{2,1,0:T(8,128)} custom-call(bf16[4,16,16384]{2,1,0:T(8,128)(2,1)} %bitcast.3, bf16[512,16384]{1,0:T(8,128)(2,1)} %hist.1, s32[4,128]{1,0:T(4,128)} %mask.1, s32[16,2]{1,0:T(8,128)} %copy.5.pairs), custom_call_target="tpu_custom_call" | custom-call | tf_op jit(solution)/shard_map/pallas_call | solution.py:480
  217.3 1.6 copy.7

commit v3 on v2

--- a/solution.py
+++ b/solution.py
@@ -12,8 +12,8 @@
 RING = 4
 UNITS = 4
 BLK = 128
-WAIT_PARTNER = 8
-WAIT_HOME = 12
+WAIT_PARTNER = 24
+WAIT_HOME = 32
 
 
 def simulate(todo, needs, rank, link, length, depth, latency=2.0, ready=()):
@@ -119,10 +119,33 @@
 
 HIST_RANK = (0, 0, 0, 0)
 DEPTH = 10
+TAIL = (4, 7, 9, 15, 27)
 GATHER = plan_gather()
 SPREAD = plan_spread()
-DIRECT = (UNITS - 1,)
-PARTS = ((0, 96), (96, 32))
+RINGED = 2
+PARTS = ((0, 112), (112, 48))
+LEVELS = 512.0
+TOP = 32767.0
+
+
+def encode(values):
+    most = jnp.maximum(jnp.max(jnp.abs(values), axis=0, keepdims=True), 1e-18)
+    level = jnp.floor(jnp.log2(most) * LEVELS) + 2.0
+    codes = jnp.round(values * (TOP * jnp.exp2(level * (-1.0 / LEVELS))))
+    return codes.astype(jnp.int32).astype(jnp.int16), level
+
+
+def level_rows(levels):
+    row = lax.broadcasted_iota(jnp.int32, (16, levels[0].shape[1]), 0)
+    tile = jnp.broadcast_to(levels[-1], row.shape)
+    for i, level in enumerate(levels[:-1]):
+        tile = jnp.where(row == i, level, tile)
+    return tile.astype(jnp.int32).astype(jnp.int16)
+
+
+def decode(codes, level):
+    step = jnp.exp2(level * (1.0 / LEVELS)) * (1.0 / TOP)
+    return codes.astype(jnp.int32).astype(jnp.float32) * step
 
 
 def numbered(order):
@@ -139,7 +162,7 @@
 
 def kernel(
     planes, hist, mask, pairs, out,
-    g_ref, h_ref, hp, acc, accp, r1, r2, r3, r4, r5, pb, d_ref, e1, e2,
+    g_ref, h_ref, hp, acc, accp, r1, r2, r3, r4, dq, r5, pb, d_ref, e1, e2,
     own_sem, hist_sem, send, recv, s1, v1, s2, v2, s3, v3, s4, v4, s5, v5, s6, v6,
     ts, tv, us, uv,
 ):
@@ -277,7 +300,12 @@
         some = g_ref[g, k].reshape(RING * RING * cols, quarter)
         dims = (((1,), (1,)), ((), ()))
         total = lax.dot_general(some, hp[k], dims, preferred_element_type=jnp.float32)
-        accp[g, k] = total.reshape(shape)
+        if g < RINGED:
+            accp[g, k] = total.reshape(shape)
+        else:
+            codes, level = encode(total)
+            dq[g - RINGED, k, 0 : codes.shape[0]] = codes
+            dq[g - RINGED, k, codes.shape[0] :] = level_rows([level])
 
     turn = {1: 0, -1: 1, 2: 2}
 
@@ -304,14 +332,17 @@
         sem = v5.at[g, c, k]
         remote(r4.at[g, c, k], r4.at[g, c, k], s5.at[g, k, c], sem, twin).wait_recv()
 
-    def direct_copy(k):
-        return remote(accp.at[UNITS - 1, k], r5.at[k], s6.at[k], v6.at[k], beside(k, PARTNER))
+    def direct_copy(g, k):
+        i = g - RINGED
+        return remote(dq.at[i, k], r5.at[i, k], s6.at[i, k], v6.at[i, k], beside(k, PARTNER))
 
     def reduce_first(g):
-        if g in DIRECT:
+        if g >= RINGED:
             for k in (0, 1):
-                direct_copy(k).wait_recv()
-            acc[g] = acc[g] + r5[0] + r5[1]
+                direct_copy(g, k).wait_recv()
+                many = RING * RING * cols
+                level = r5[g - RINGED, k, many:].astype(jnp.int32).astype(jnp.float32)[0:1]
+                acc[g] = acc[g] + decode(r5[g - RINGED, k, 0:many], level).reshape(shape)
         pair_copy(g).start()
 
     def reduce_second(g):
@@ -321,7 +352,7 @@
             ring_copy(g, d).start()
 
     def reduce_partner(g):
-        if g in DIRECT:
+        if g >= RINGED:
             return
         for k in (0, 1):
             for d in (1, -1, 2):
@@ -334,13 +365,24 @@
         for d in (1, -1, 2):
             ring_copy(g, d).wait_recv()
         total = acc[g, y, core] + r2[g, 0] + r2[g, 1] + r2[g, 2]
-        if g not in DIRECT:
+        if g < RINGED:
             for k in (0, 1):
                 for c in (0, 1):
                     home_wait(g, k, c)
                     total = total + r4[g, c, k]
+        codes, level = encode(total)
+        levels.append(level)
+        last_of = g >= UNITS - 2
+        at = g * 32 if g < UNITS - 1 else PARTS[1][0]
+        tile = level_rows(levels[-1:] if g == UNITS - 1 else levels) if last_of else None
         for b in range(4):
-            pb[me * RING + b, pl.ds(g * 32, 32)] = total[:, b * BLK : (b + 1) * BLK]
+            some = slice(b * BLK, (b + 1) * BLK)
+            pb[me * RING + b, at : at + 32] = codes[:, some]
+            if last_of:
+                end = at + 32
+                pb[me * RING + b, end : end + 16] = tile[:, some]
+
+    levels = []
 
     def spread_steps(h, begin, end):
         for c, started in SPREAD[begin:end]:
@@ -351,7 +393,7 @@
 
     got = {u: 1.0 for u in range(2 * UNITS)}
     tiles = {0: 0, 1: 0}
-    waiting, seen, later = [], set(), []
+    waiting, seen, later, held = [], set(), [], []
     steps = len(SPREAD)
     last = max(n for n, (_, started) in enumerate(GATHER) if started)
     for n, (c, started) in enumerate(GATHER):
@@ -383,37 +425,52 @@
             waiting.remove(u)
             g, k = u // 2, u % 2
             multiply_partner(g, k)
-            if g in DIRECT:
-                direct_copy(k).start()
+            if g >= RINGED:
+                direct_copy(g, k).start()
             else:
                 for d in (2, 1, -1):
                     partner_ring(g, k, d).start()
+            if g == UNITS - 1:
+                held.append(k)
+                continue
             multiply(g, k, g not in seen)
-            if g in seen:
-                if g in DIRECT:
-                    assert n >= len(GATHER) - 4
-                    later.append((n, lambda g=g: reduce_first(g)))
-                else:
-                    reduce_first(g)
+            if g in seen and g >= RINGED:
+                later.append((n + 6, lambda g=g: reduce_first(g)))
+                later.append((n + 10, lambda g=g: reduce_second(g)))
+                later.append((n + 17, lambda g=g: reduce_third(g)))
+            elif g in seen:
+                reduce_first(g)
                 later.append((n + 4, lambda g=g: reduce_second(g)))
                 later.append((n + WAIT_PARTNER, lambda g=g: reduce_partner(g)))
                 later.append((n + WAIT_HOME, lambda g=g: reduce_third(g)))
             seen.add(g)
 
-    later.sort(key=lambda e: e[0])
-    assert not waiting and len(later) == 4
-    later.pop(0)[1]()
-    spread_steps(0, 1, 9)
-    later[0][1]()
-    spread_steps(0, 9, 25)
-    later[2][1]()
+    assert not waiting and not later and len(held) == 2
+    g = UNITS - 1
+    spread_steps(0, 1, TAIL[0])
+    multiply(g, held[0], True)
+    spread_steps(0, TAIL[0], TAIL[1])
+    multiply(g, held[1], False)
+    spread_steps(0, TAIL[1], TAIL[2])
+    reduce_first(g)
+    spread_steps(0, TAIL[2], TAIL[3])
+    reduce_second(g)
+    spread_steps(0, TAIL[3], TAIL[4])
+    reduce_third(g)
     spread_steps(1, 0, 1)
-    spread_steps(0, 25, steps)
+    spread_steps(0, TAIL[4], steps)
     spread_steps(1, 1, steps)
 
     def one_pair(k, _):
-        lt = pb[pairs[k, 0]]
-        rt = pb[pairs[k, 1]]
+        def block(i):
+            level = pb[i, 96:112].astype(jnp.int32).astype(jnp.float32)
+            out = [decode(pb[i, g * 32 : (g + 1) * 32], level[g : g + 1]) for g in range(3)]
+            level = pb[i, 144:160].astype(jnp.int32).astype(jnp.float32)
+            out.append(decode(pb[i, 112:144], level[0:1]))
+            return jnp.concatenate(out, axis=0)
+
+        lt = block(pairs[k, 0])
+        rt = block(pairs[k, 1])
         dots = lax.dot_general(
             lt, rt, (((0,), (0,)), ((), ())),
             precision=lax.Precision.HIGHEST, preferred_element_type=jnp.float32,
@@ -460,8 +517,8 @@
         for d in (1, -1, 2):
             ring_copy(g, d).wait_send()
         for k in (0, 1):
-            if g in DIRECT:
-                direct_copy(k).wait_send()
+            if g >= RINGED:
+                direct_copy(g, k).wait_send()
                 continue
             for d in (1, -1, 2):
                 partner_ring(g, k, d).wait_send()
@@ -492,13 +549,14 @@
             pltpu.VMEM((rows, depth), jnp.bfloat16),
             pltpu.VMEM((2, rows, depth // 4), jnp.bfloat16),
             pltpu.VMEM((UNITS, RING, 2, 2 * cols, rows), f32),
-            pltpu.VMEM((UNITS, 2, RING, 2, 2 * cols, rows), f32),
+            pltpu.VMEM((RINGED, 2, RING, 2, 2 * cols, rows), f32),
             pltpu.VMEM((UNITS, RING, 2 * cols, rows), f32),
             pltpu.VMEM((UNITS, 3, 2 * cols, rows), f32),
-            pltpu.VMEM((UNITS - 1, 2, 3, 2, 2 * cols, rows), f32),
-            pltpu.VMEM((UNITS - 1, 2, 2, 2 * cols, rows), f32),
-            pltpu.VMEM((2, RING, 2, 2 * cols, rows), f32),
-            pltpu.VMEM((RING * RING * RING, BLK, BLK), f32),
+            pltpu.VMEM((RINGED, 2, 3, 2, 2 * cols, rows), f32),
+            pltpu.VMEM((RINGED, 2, 2, 2 * cols, rows), f32),
+            pltpu.VMEM((UNITS - RINGED, 2, RING * RING * cols + 16, rows), jnp.int16),
+            pltpu.VMEM((UNITS - RINGED, 2, RING * RING * cols + 16, rows), jnp.int16),
+            pltpu.VMEM((RING * RING * RING, 160, BLK), jnp.int16),
             pltpu.VMEM((2, RING, 2, BLK + 16, BLK), f32),
             pltpu.VMEM((RING, 2, BLK + 16, BLK), f32),
             pltpu.VMEM((3, 2, BLK + 16, BLK), f32),
@@ -512,12 +570,12 @@
             dma((UNITS, 3)),
             dma,
             dma,
-            dma((UNITS - 1, 2, 3)),
-            dma((UNITS - 1, 2, 3)),
-            dma((UNITS - 1, 2, 2)),
-            dma((UNITS - 1, 2, 2)),
-            dma((2,)),
-            dma((2,)),
+            dma((RINGED, 2, 3)),
+            dma((RINGED, 2, 3)),
+            dma((RINGED, 2, 2)),
+            dma((RINGED, 2, 2)),
+            dma((UNITS - RINGED, 2)),
+            dma((UNITS - RINGED, 2)),
             dma((2, len(SPREAD_IDS))),
             dma((2, len(SPREAD_IDS))),
             dma((3,)),

time: 219 us -> 203 us (0.927)
  Pallas kernels: 216 us -> 200 us
    pallas_call x1, Pallas kernels: 216 us -> 200 us  [body(): pl.pallas_call(kernel, out_shape=jax.ShapeDtypeStruct((2, BLK, BLK), f32)...]
where the time goes in v3:
time: 203 us
  Pallas kernels  200 us (99%)
  local copies, waits for them, and re-layouts  2.92 us (1%)
    pallas_call x1, Pallas kernels, body(): pl.pallas_call(kernel, out_shape=jax.ShapeDtypeStruct((2, BLK, BLK), f32)...  200 us

profile of v3, /device:TPU:1, one launch (start us, length us, event | category | flops | bytes accessed | tf_op | source)
XLA Modules:
  0.0 202.8 jit_solution(12207051992177830881)
XLA Ops:
  0.0 1.4 copy.5.pairs
  1.4 199.9 %shard_map.46 = f32[2,128,128]{2,1,0:T(8,128)} custom-call(bf16[4,16,16384]{2,1,0:T(8,128)(2,1)} %bitcast.3, bf16[512,16384]{1,0:T(8,128)(2,1)} %hist.1, s32[4,128]{1,0:T(4,128)} %mask.1, s32[16,2]{1,0:T(8,128)} %copy.5.pairs), custom_call_target="tpu_custom_call" | custom-call | tf_op jit(solution)/shard_map/pallas_call | solution.py:537
  201.3 1.6 copy.7

commit v4 on v3

--- a/solution.py
+++ b/solution.py
@@ -12,8 +12,8 @@
 RING = 4
 UNITS = 4
 BLK = 128
-WAIT_PARTNER = 24
-WAIT_HOME = 32
+WAIT_PARTNER = 32
+WAIT_HOME = 42
 
 
 def simulate(todo, needs, rank, link, length, depth, latency=2.0, ready=()):
@@ -124,12 +124,12 @@
 SPREAD = plan_spread()
 RINGED = 2
 PARTS = ((0, 112), (112, 48))
-LEVELS = 512.0
+LEVELS = 256.0
 TOP = 32767.0
 
 
 def encode(values):
-    most = jnp.maximum(jnp.max(jnp.abs(values), axis=0, keepdims=True), 1e-18)
+    most = jnp.maximum(jnp.max(jnp.abs(values), axis=0, keepdims=True), 1e-33)
     level = jnp.floor(jnp.log2(most) * LEVELS) + 2.0
     codes = jnp.round(values * (TOP * jnp.exp2(level * (-1.0 / LEVELS))))
     return codes.astype(jnp.int32).astype(jnp.int16), level
@@ -162,7 +162,7 @@
 
 def kernel(
     planes, hist, mask, pairs, out,
-    g_ref, h_ref, hp, acc, accp, r1, r2, r3, r4, dq, r5, pb, d_ref, e1, e2,
+    g_ref, h_ref, hp, acc, accp, r1, r2, r3, r4, dq, r5, pb, d_ref, e1, dt, e2,
     own_sem, hist_sem, send, recv, s1, v1, s2, v2, s3, v3, s4, v4, s5, v5, s6, v6,
     ts, tv, us, uv,
 ):
@@ -435,9 +435,9 @@
                 continue
             multiply(g, k, g not in seen)
             if g in seen and g >= RINGED:
-                later.append((n + 6, lambda g=g: reduce_first(g)))
-                later.append((n + 10, lambda g=g: reduce_second(g)))
-                later.append((n + 17, lambda g=g: reduce_third(g)))
+                later.append((n + 10, lambda g=g: reduce_first(g)))
+                later.append((n + 15, lambda g=g: reduce_second(g)))
+                later.append((n + 21, lambda g=g: reduce_third(g)))
             elif g in seen:
                 reduce_first(g)
                 later.append((n + 4, lambda g=g: reduce_second(g)))
@@ -461,7 +461,9 @@
     spread_steps(0, TAIL[4], steps)
     spread_steps(1, 1, steps)
 
-    def one_pair(k, _):
+    def one_pair(c, i):
+        k = 4 * (i // 2) + 2 * c + i % 2
+
         def block(i):
             level = pb[i, 96:112].astype(jnp.int32).astype(jnp.float32)
             out = [decode(pb[i, g * 32 : (g + 1) * 32], level[g : g + 1]) for g in range(3)]
@@ -475,37 +477,50 @@
             lt, rt, (((0,), (0,)), ((), ())),
             precision=lax.Precision.HIGHEST, preferred_element_type=jnp.float32,
         )
-        at = d_ref.at[(k // 2) % 2, k // 4, k % 2]
+        at = d_ref.at[c, i // 2, i % 2]
         at[0:BLK] = dots
         at[BLK : BLK + 8] = jnp.broadcast_to(jnp.sum(lt * lt, axis=0, keepdims=True), (8, BLK))
         at[BLK + 8 : BLK + 16] = jnp.broadcast_to(jnp.sum(rt * rt, axis=0, keepdims=True), (8, BLK))
         return 0
 
-    lax.fori_loop(0, pairs.shape[0], one_pair, 0, unroll=4)
+    def pairs_of(c):
+        return lax.fori_loop(0, pairs.shape[0] // 2, lambda i, _: one_pair(c, i), 0, unroll=8)
+
+    pairs_of(1 - core)
     swap = remote(d_ref.at[1 - core], e1, s3, v3, twin)
     swap.start()
+    pairs_of(core)
     swap.wait_recv()
 
-    def add(i, _):
-        d_ref[core, i] = d_ref[core, i] + e1[i]
-        return 0
-
-    lax.fori_loop(0, RING, add, 0)
-
     def share_copy(d):
-        i = {1: 0, -1: 1, 2: 2}[d]
-        return remote(d_ref.at[core, wrap(y, d)], e2.at[i], us.at[i], uv.at[i], along_y(d))
+        i = turn[d]
+        return remote(dt.at[i], e2.at[i], us.at[i], uv.at[i], along_y(d))
 
     for d in (2, 1, -1):
+        i, there = turn[d], wrap(y, d)
+        for j in range(2):
+            total = d_ref[core, there, j] + e1[there, j]
+            codes, level = encode(total[0:BLK])
+            square_codes, square_level = encode(total[BLK:])
+            dt[i, j, 0:BLK] = codes
+            dt[i, j, BLK : BLK + 16] = square_codes
+            dt[i, j, BLK + 16 :] = level_rows([level, square_level])
         share_copy(d).start()
+    totals = [d_ref[core, y, j] + e1[y, j] for j in range(2)]
+    dots = [t[0:BLK] for t in totals]
+    squares = [t[BLK:] for t in totals]
     for d in (1, -1, 2):
+        i = turn[d]
         share_copy(d).wait_recv()
+        for j in range(2):
+            level = e2[i, j, BLK + 16 :].astype(jnp.int32).astype(jnp.float32)
+            dots[j] = dots[j] + decode(e2[i, j, 0:BLK], level[0:1])
+            squares[j] = squares[j] + decode(e2[i, j, BLK : BLK + 16], level[1:2])
     for j in range(2):
-        total = d_ref[core, y, j] + e2[0, j] + e2[1, j] + e2[2, j]
-        lscale = lax.rsqrt(total[BLK : BLK + 1] / P_SIZE + 1e-06)
-        rscale = lax.rsqrt(total[BLK + 8 : BLK + 9] / P_SIZE + 1e-06)
+        lscale = lax.rsqrt(squares[j][0:1] / P_SIZE + 1e-06)
+        rscale = lax.rsqrt(squares[j][8:9] / P_SIZE + 1e-06)
         lfull = jnp.broadcast_to(lscale, (BLK, BLK)).T
-        out[j] = total[0:BLK] / P_SIZE * lfull * rscale
+        out[j] = dots[j] / P_SIZE * lfull * rscale
 
     for c in GATHER_IDS:
         gather_copy(c).wait_send()
@@ -559,7 +574,8 @@
             pltpu.VMEM((RING * RING * RING, 160, BLK), jnp.int16),
             pltpu.VMEM((2, RING, 2, BLK + 16, BLK), f32),
             pltpu.VMEM((RING, 2, BLK + 16, BLK), f32),
-            pltpu.VMEM((3, 2, BLK + 16, BLK), f32),
+            pltpu.VMEM((3, 2, BLK + 32, BLK), jnp.int16),
+            pltpu.VMEM((3, 2, BLK + 32, BLK), jnp.int16),
             dma((2,)),
             dma((4,)),
             dma((len(GATHER_IDS),)),

time: 203 us -> 197 us (0.970)
  Pallas kernels: 200 us -> 194 us
    pallas_call x1, Pallas kernels: 200 us -> 194 us  [body(): pl.pallas_call(kernel, out_shape=jax.ShapeDtypeStruct((2, BLK, BLK), f32)...]
where the time goes in v4:
time: 197 us
  Pallas kernels  194 us (98%)
  local copies, waits for them, and re-layouts  2.92 us (1%)
    pallas_call x1, Pallas kernels, body(): pl.pallas_call(kernel, out_shape=jax.ShapeDtypeStruct((2, BLK, BLK), f32)...  194 us

profile of v4, /device:TPU:1, one launch (start us, length us, event | category | flops | bytes accessed | tf_op | source)
XLA Modules:
  0.0 197.0 jit_solution(10959476714403227160)
XLA Ops:
  0.0 1.4 copy.5.pairs
  1.4 194.1 %shard_map.46 = f32[2,128,128]{2,1,0:T(8,128)} custom-call(bf16[4,16,16384]{2,1,0:T(8,128)(2,1)} %bitcast.3, bf16[512,16384]{1,0:T(8,128)(2,1)} %hist.1, s32[4,128]{1,0:T(4,128)} %mask.1, s32[16,2]{1,0:T(8,128)} %copy.5.pairs), custom_call_target="tpu_custom_call" | custom-call | tf_op jit(solution)/shard_map/pallas_call | solution.py:552
  195.4 1.6 copy.7
